TPU v7x, 32 devices: a whole 2x2x4 slice. The times are simulated.
32 devices in a mesh: row: 4 (over y, x), col: 8 (over z, core).
Axes of the slice: x: 2, y: 2, z: 4, core: 2. Of those that a mesh axis runs over, the one named last changes fastest.
Arguments:
- throat_owner: int32 [16384, 1], P(('row', 'col')), may hold values from 0 to 3; in each aligned block of 512 rows (0 to 511, 512 to 1023, ...) at most 128 rows name the same one
- throat_interior: int32 [16384], P(('row', 'col')), may hold values from 0 to 895
- throat_offset: int32 [16384], P(('row', 'col')), may hold values from 0 to 4095
- throat_conductance: float32 [16384], P(('row', 'col')), may hold values from 0.1 to 1
- child_update: bfloat16 [7168, 16384], P('col', 'row'), may hold values from -0.09375 to 0.09375
- panel_pores: int32 [4096], replicated, may hold values from 0 to 16383, as said below
- interior_inverse: bfloat16 [7168, 896], P('col'), as said below
- separator_rows: float32 [4096, 16384], P('col', 'row'), may hold values from -6 to 6
Outputs:
- schur_rows: float32 [4096, 16384], P('col', 'row')
Inputs may be any that keep to these rules, and one draw needn't show every extreme that they name: `throat_owner`: in each device's block of 512 throats no owner is named more than 128 times, a bound that some block reaches. `panel_pores`: the 4096 pores are distinct; at most 1536 of them lie in any one owner's range of 4096 pores, and one owner holds exactly 1536. `interior_inverse`: each group's block of 896 rows is lower triangular with diagonal entries between 0.8 and 1.2.
All inputs are finite; a program needn't handle non-finite values.
Results may differ from a plain program's by a relative error of at most 0.01.
Values may be sent and summed in bfloat16 or wider, within the bound.
No kernel may reach another device: no remote copies, remote signals or barrier semaphores. Data moves between devices by JAX's collectives and lax.ppermute only.
A program may use at most 128 MiB of HBM per device.

v0:
```python
import jax
import jax.numpy as jnp
from jax import lax
from jax.sharding import PartitionSpec as P


def rank_within(owners, owner_count):
    onehot = (owners[:, None] == jnp.arange(owner_count, dtype=jnp.int32)[None, :]).astype(
        jnp.int32
    )
    before = jnp.cumsum(onehot, axis=0) - onehot
    return jnp.sum(before * onehot, axis=1)


def panel_slots(panel_pores, owner_width, row_count, row_index):
    panel_total = panel_pores.shape[0]
    panel_owner = panel_pores // owner_width
    panel_within = rank_within(panel_owner, row_count)
    panel_limit = 3 * panel_total // (2 * row_count)
    picked = jnp.where(panel_owner == row_index, panel_within, panel_limit)
    chosen = (
        jnp.zeros((panel_limit,), jnp.int32)
        .at[picked]
        .set(panel_pores - panel_owner * owner_width, mode="drop")
    )
    placed = panel_owner * panel_limit + panel_within
    return (chosen, placed)


def per_device(
    throat_owner,
    throat_interior,
    throat_offset,
    throat_conductance,
    child_update,
    panel_pores,
    interior_inverse,
    separator_rows,
):
    row_count = lax.axis_size("row")
    row_index = lax.axis_index("row")
    owner_width = separator_rows.shape[1]
    throats = throat_interior.shape[0]
    slot_limit = throats // 4
    owners = throat_owner[:, 0]
    slot_ids = owners * slot_limit + rank_within(owners, row_count)
    total_slots = row_count * slot_limit
    rows_sent = jnp.zeros((total_slots,), jnp.int32).at[slot_ids].set(throat_interior)
    cols_sent = jnp.zeros((total_slots,), jnp.int32).at[slot_ids].set(throat_offset)
    values_sent = jnp.zeros((total_slots,), jnp.float32).at[slot_ids].set(throat_conductance)
    index_block = jnp.stack(
        [rows_sent.reshape(row_count, slot_limit), cols_sent.reshape(row_count, slot_limit)], axis=1
    )
    index_back, values_back = (
        lax.all_to_all(index_block, "row", split_axis=0, concat_axis=0, tiled=True),
        lax.all_to_all(
            values_sent.reshape(row_count, slot_limit),
            "row",
            split_axis=0,
            concat_axis=0,
            tiled=True,
        ),
    )
    summed = (
        child_update.astype(jnp.float32)
        .at[index_back[:, 0, :].ravel(), index_back[:, 1, :].ravel()]
        .add(values_back.ravel())
    )
    coupling = summed.astype(jnp.bfloat16)
    solved = jnp.dot(interior_inverse, coupling, preferred_element_type=jnp.float32).astype(
        jnp.bfloat16
    )
    chosen, placed = panel_slots(panel_pores, owner_width, row_count, row_index)
    local_columns = jnp.take(solved, chosen, axis=1)
    gathered = lax.all_gather(local_columns, "row", axis=1, tiled=True)
    panel_solved = jnp.take(gathered, placed, axis=1)
    update = lax.psum_scatter(
        jnp.dot(panel_solved.T, solved, preferred_element_type=jnp.float32).astype(jnp.bfloat16),
        "col",
        scatter_dimension=0,
        tiled=True,
    ).astype(jnp.float32)
    return separator_rows - update


def solution(mesh):
    in_specs = (
        P(("row", "col"), None),
        P(("row", "col")),
        P(("row", "col")),
        P(("row", "col")),
        P("col", "row"),
        P(),
        P("col", None),
        P("col", "row"),
    )
    out_specs = P("col", "row")
    return jax.shard_map(
        per_device, mesh=mesh, in_specs=in_specs, out_specs=out_specs, check_vma=False
    )
```

profile of v0, /device:TPU:0, one launch (start us, length us, event | category | flops | bytes accessed | tf_op | source)
XLA Modules:
  0.0 674.5 jit_solution(6133341720263990972)
XLA Ops:
  6.5 0.0 copy-start
  6.5 0.8 fusion.17
  7.3 1.2 reduce-window.16
  8.6 0.2 slice_reduce_fusion.1
  8.8 0.2 reduce-window.19
  8.9 0.1 add_bitcast_fusion.1
  9.0 0.7 fusion.16
  9.7 0.7 compare_select_fusion.5
  10.4 2.6 scatter_custom_fusion.2
  13.0 2.6 scatter_custom_fusion.1
  15.6 0.6 pad_add_fusion
  16.2 5.2 all-to-all-start
  21.4 0.7 add_select_fusion
  22.1 1.2 reduce-window.14
  23.3 0.2 slice_reduce_fusion
  23.5 0.2 reduce-window.15
  23.7 0.1 add_bitcast_fusion
  23.8 0.1 fusion.10
  23.9 0.7 broadcast_clamp_fusion
  24.7 15.5 %scatter_custom_fusion = s32[1536]{0:T(1024)S(1)} fusion(s32[4096]{0:T(1024)S(1)} %get-tuple-element.6, s32[4096]{0:T(1024)S(1)} %get-tuple-element.7, s32[]{:T(128)} %constant.39.clone.1), kind=kCustom, calls=%fused_computation.54 | custom fusion | bytes 6148 | tf_op jit(solution)/shard_map/scatter | solution.py:24
  40.2 10.3 %convert_element_type.34 = f32[896,4096]{1,0:T(8,128)} convert(bf16[896,4096]{1,0:T(8,128)(2,1)} %param.12) | non-fusion elementwise | flops 3670016 | bytes 22020096 | tf_op jit(solution)/shard_map/convert_element_type | solution.py:65
  50.5 3.2 scatter_custom_fusion.3
  53.7 0.0 all-to-all-done
  53.7 4.2 all-to-all-start.1
  57.9 0.0 all-gather.2.cloned.1.call-start
  57.9 4.5 all-to-all-done.1
  62.4 61.4 %scatter_fusion = f32[896,4096]{1,0:T(8,128)} fusion(f32[896,4096]{1,0:T(8,128)} %convert_element_type.34, s32[512]{0:T(512)S(1)} %bitcast.67, f32[512]{0:T(512)S(1)} %bitcast.70), kind=kCustom, calls=%fused_computation.6 | custom fusion | flops 512 | bytes 10240 | tf_op jit(solution)/shard_map/scatter-add | solution.py:67
  123.8 0.0 copy-done
  123.8 16.0 %fusion.4 = bf16[4096,896]{1,0:T(8,128)(2,1)} fusion(bf16[896,896]{1,0:T(8,128)(2,1)S(1)} %copy-done, f32[896,4096]{1,0:T(8,128)} %scatter_fusion), kind=kOutput, calls=%fused_computation.13 | convolution fusion | flops 6584008704 | bytes 23625728 | tf_op jit(solution)/shard_map/dot_general | solution.py:70
  139.9 11.1 %gather_fusion = bf16[1536,896]{1,0:T(8,128)(2,1)} fusion(bf16[896,4096]{0,1:T(8,128)(2,1)} %bitcast.66, s32[2048]{0:T(1024)S(1)} %pad_clamp_fusion), kind=kCustom, calls=%fused_computation | custom fusion | bytes 5511168 | tf_op jit(solution)/shard_map/jit(_take)/gather | solution.py:74
  151.0 0.0 copy-start.2
  151.0 3.8 select_bitcast_fusion
  154.8 0.0 all-gather.2.cloned.1.call-update
  154.8 0.3 reduce-scatter.2.cloned.1.call-start
  155.1 0.0 copy-done.2
  155.1 108.7 %all-gather.2.cloned.1.call-done = bf16[896,6144]{0,1:T(8,128)(2,1)} async-done(((bf16[896,1536]{0,1:T(8,128)(2,1)}), bf16[896,6144]{0,1:T(8,128)(2,1)}) %all-gather.2.cloned.1.call-update) | async-done | bytes 11010064 | tf_op jit(solution)/shard_map/all_gather | solution.py:75
  263.8 25.3 %gather_fusion.1 = bf16[4096,896]{1,0:T(8,128)(2,1)} fusion(bf16[896,6144]{0,1:T(8,128)(2,1)} %all-gather.2.cloned.1.call-done, s32[4096]{0:T(1024)S(1)} %get-tuple-element.5), kind=kCustom, calls=%fused_computation.1 | custom fusion | bytes 14696448 | tf_op jit(solution)/shard_map/jit(_take)/gather | solution.py:76
  289.1 43.1 %convolution_convert_fusion = bf16[4096,4096]{1,0:T(8,128)(2,1)} fusion(bf16[4096,896]{1,0:T(8,128)(2,1)} %fusion.4, bf16[4096,896]{1,0:T(8,128)(2,1)} %gather_fusion.1, pred[4096]{0:T(1024)(128)(4,1)S(1)} %compare_and_fusion), kind=kOutput, calls=%fused_computation.7 | convolution fusion | flops 30085218304 | bytes 48238592 | tf_op jit(solution)/shard_map/dot_general | solution.py:78
  332.2 0.0 reduce-scatter.2.cloned.1.call-update
  332.2 0.0 copy-start.1
  332.3 325.7 %reduce-scatter.2.cloned.1.call-done = bf16[512,4096]{1,0:T(8,128)(2,1)} async-done(((bf16[4096,4096]{1,0:T(8,128)(2,1)}), bf16[512,4096]{1,0:T(8,128)(2,1)}) %reduce-scatter.2.cloned.1.call-update) | async-done | bytes 4194320 | tf_op jit(solution)/shard_map/reduce_scatter | solution.py:77
  657.9 9.7 %convert_subtract_fusion = f32[512,4096]{1,0:T(8,128)} fusion(f32[512,4096]{1,0:T(8,128)} %param.15, bf16[512,4096]{1,0:T(8,128)(2,1)} %reduce-scatter.2.cloned.1.call-done), kind=kLoop, calls=%fused_computation.8 | loop fusion | flops 4194304 | bytes 20971520 | tf_op jit(solution)/shard_map/sub | solution.py:83
  667.6 0.0 copy-done.1
  (6 shorter events, 0.1 us)
Async XLA Ops:
  6.5 117.3 %copy-start = (bf16[896,896]{1,0:T(8,128)(2,1)S(1)}, bf16[896,896]{1,0:T(8,128)(2,1)}, u32[]{:S(2)}) copy-start(bf16[896,896]{1,0:T(8,128)(2,1)} %param.14) | copy-start | bytes 4816900
  16.2 37.5 %all-to-all-start = ((s32[4,2,128]{2,1,0:T(2,128)}), s32[4,2,128]{2,1,0:T(2,128)S(1)}, u32[]{:S(2)}, u32[]{:S(2)}) async-start(s32[4,2,128]{2,1,0:T(2,128)} %pad_add_fusion), calls=%async_computation | async-start | bytes 8192 | tf_op jit(solution)/shard_map/all_to_all | solution.py:55
  53.7 8.7 %all-to-all-start.1 = ((f32[4,1,128]{2,1,0:T(1,128)}), f32[4,1,128]{2,1,0:T(1,128)S(1)}, u32[]{:S(2)}, u32[]{:S(2)}) async-start(f32[4,1,128]{2,1,0:T(1,128)} %bitcast.12), calls=%async_computation.1 | async-start | bytes 4096 | tf_op jit(solution)/shard_map/all_to_all | solution.py:56
  57.9 205.9 %all-gather.2.cloned.1.call-start = ((), (), s32[]{:S(2)}) async-start(), calls=%async_computation.3 | async-start | bytes 13762560 | tf_op jit(solution)/shard_map/all_gather | solution.py:75
  151.0 4.1 copy-start.2
  154.8 503.1 %reduce-scatter.2.cloned.1.call-start = ((), (), s32[]{:S(2)}) async-start(), calls=%async_computation.4 | async-start | bytes 37748736 | tf_op jit(solution)/shard_map/reduce_scatter | solution.py:77
  332.2 335.4 %copy-start.1 = (bf16[896,896]{1,0:T(8,128)(2,1)S(1)}, bf16[896,896]{1,0:T(8,128)(2,1)}, u32[]{:S(2)}) copy-start(bf16[896,896]{1,0:T(8,128)(2,1)} %param.14) | copy-start | bytes 4816900
Sparse Core Ops, SparseCore 0:
  155.0 108.8 all-gather.1
  332.4 325.5 reduce-scatter.1
where the time goes:
time: 677 us; the launch traced here: 674 us
  waiting for transfers between devices  439 us (65%)
  other arithmetic  92.6 us (14%)
  local copies, waits for them, and re-layouts  60.7 us (9%)
  matrix products  59.1 us (9%)
  between operations  13.5 us (2%)
  starting transfers between devices  9.62 us (1%)
    reduce_scatter x1, waiting for transfers between devices, per_device(): lax.psum_scatter(jnp.dot(panel_solved.T, solved, preferred_element_type=j...  326 us
    all_gather x1, waiting for transfers between devices, per_device(): gathered = lax.all_gather(local_columns, 'row', axis=1, tiled=True)  109 us
    scatter-add x1, other arithmetic, per_device(): summed = child_update.astype(jnp.float32).at[index_back[:, 0, :].ravel(),...  61.4 us
    dot_general x1, matrix products, per_device(): jnp.dot(panel_solved.T, solved, preferred_element_type=jnp.float32)  43.1 us
    gather x1, local copies, waits for them, and re-layouts, per_device(): panel_solved = jnp.take(gathered, placed, axis=1)  25.3 us
    dot_general x1, matrix products, per_device(): jnp.dot(interior_inverse, coupling, preferred_element_type=jnp.float32)  16 us
    scatter x1, local copies, waits for them, and re-layouts, panel_slots(): chosen = jnp.zeros((panel_limit,), jnp.int32).at[picked].set(panel_pores...  15.5 us
  transfers between devices with their start and end apart: 4, of which 3 were waited for; matrix products, arithmetic and copies ran while one was open for 5% of the time, Pallas kernels for 0%

commit v1 on v0

v1 whole, which is shorter than its diff:
```python
import jax
import jax.numpy as jnp
from jax import lax
from jax.sharding import PartitionSpec as P

STEPS = (2, 3, 3, 4, 5, 6, 5, 3, 1)


def route_throats(owners, interior, offset, conductance, row_count, owner_width):
    throats = interior.shape[0]
    slot_limit = throats // 4
    order = jnp.arange(throats, dtype=jnp.int32)
    earlier = (owners[None, :] == owners[:, None]) & (order[None, :] < order[:, None])
    rank = jnp.sum(earlier.astype(jnp.int32), axis=1)
    slot = owners * slot_limit + rank
    code = (interior * owner_width + offset + 1).astype(jnp.float32)
    slots = jnp.arange(row_count * slot_limit, dtype=jnp.int32)
    placed = slots[:, None] == slot[None, :]
    codes = jnp.sum(jnp.where(placed, code[None, :], 0.0), axis=1)
    values = jnp.sum(jnp.where(placed, conductance[None, :], 0.0), axis=1)
    block = jnp.stack(
        [codes.reshape(row_count, slot_limit), values.reshape(row_count, slot_limit)], axis=1
    )
    back = lax.all_to_all(block, "row", split_axis=0, concat_axis=0, tiled=True)
    codes = back[:, 0, :].reshape(-1).astype(jnp.int32) - 1
    values = back[:, 1, :].reshape(-1)
    return codes // owner_width, codes % owner_width, values


def add_throats(child_update, pivots, pores, values):
    high = lax.reduce_precision(values, 8, 7)
    low = values - high
    values = jnp.concatenate([high, low]).astype(jnp.bfloat16)
    pivots = jnp.concatenate([pivots, pivots])
    pores = jnp.concatenate([pores, pores])
    rows = jnp.arange(child_update.shape[0], dtype=jnp.int32)
    columns = jnp.arange(child_update.shape[1], dtype=jnp.int32)
    left = jnp.where(rows[:, None] == pivots[None, :], values[None, :], jnp.bfloat16(0))
    right = (pores[:, None] == columns[None, :]).astype(jnp.bfloat16)
    summed = jnp.dot(left, right, preferred_element_type=jnp.float32)
    return (child_update.astype(jnp.float32) + summed).astype(jnp.bfloat16)


def per_device(
    throat_owner,
    throat_interior,
    throat_offset,
    throat_conductance,
    child_update,
    panel_pores,
    interior_inverse,
    separator_rows,
):
    row_count = lax.axis_size("row")
    col_count = lax.axis_size("col")
    row_index = lax.axis_index("row")
    col_index = lax.axis_index("col")
    own_rows, owner_width = separator_rows.shape
    chips = col_count // 2
    core = col_index % 2
    chip = col_index // 2
    square = row_count == 4
    line = chips == 4
    at_end = (chip == 0) | (chip == chips - 1)

    pivots, pores, values = route_throats(
        throat_owner[:, 0],
        throat_interior,
        throat_offset,
        throat_conductance,
        row_count,
        owner_width,
    )
    coupling = add_throats(child_update, pivots, pores, values)
    solved = jnp.dot(interior_inverse, coupling, preferred_element_type=jnp.float32).astype(
        jnp.bfloat16
    )

    local_pores = (panel_pores - row_index * owner_width).reshape(chips, 2, own_rows)
    if line:
        order = jnp.array([[0, 1, 2, 3], [1, 2, 3, 0], [2, 1, 0, 3], [3, 2, 1, 0]], jnp.int32)
        local_pores = jnp.take(local_pores, order[chip], axis=0)
    other_pores = jnp.where(core == 0, local_pores[:, 1], local_pores[:, 0])
    mine_pores = jnp.where(core == 0, local_pores[:, 0], local_pores[:, 1])
    columns = jnp.arange(owner_width, dtype=jnp.int32)

    swap = [(i, i ^ 1) for i in range(col_count)]
    along_x = [(i, i ^ 1) for i in range(row_count)]
    along_y = [(i, i ^ 2) for i in range(row_count)]
    ends = [(i, i ^ 2) for i in range(col_count)]
    outward = [(2 * g + c, 2 * t + c) for g, t in ((1, 0), (2, 3)) for c in range(2)]
    across = [(2 * g + c, 2 * t + c) for g, t in ((0, 0), (1, 2), (2, 1), (3, 3)) for c in range(2)]

    sizes = [own_rows * s // sum(STEPS) for s in STEPS]
    starts = [sum(sizes[:i]) for i in range(len(sizes))]
    count = len(sizes)
    state = [dict() for _ in sizes]

    def pick(s, k):
        part = slice(starts[k], starts[k] + sizes[k])
        parts = [other_pores[:, part].reshape(-1), mine_pores[:, part].reshape(-1)]
        onehot = (jnp.concatenate(parts)[:, None] == columns[None, :]).astype(jnp.bfloat16)
        rows = lax.dot_general(
            onehot, shared["solved"], (((1,), (1,)), ((), ())), preferred_element_type=jnp.float32
        ).astype(jnp.bfloat16)
        half = chips * sizes[k]
        s["first"], s["second"] = rows[:half], rows[half:]

    def share(s, k):
        if square:
            s["first_in"] = lax.ppermute(s["first"], "row", along_x)
            s["second_in"] = lax.ppermute(s["second"], "row", along_y)
        else:
            s["first"] = lax.psum(s["first"], "row")
            s["second"] = lax.psum(s["second"], "row")

    def share_again(s, k):
        if square:
            s["first"] += s.pop("first_in")
            s["second"] += s.pop("second_in")
            s["first_in"] = lax.ppermute(s["first"], "row", along_y)
            s["second_in"] = lax.ppermute(s["second"], "row", along_x)

    def multiply(s, k):
        first, second = s.pop("first"), s.pop("second")
        if square:
            first += s.pop("first_in")
            second += s.pop("second_in")
        sent, mine = (
            jnp.dot(rows, shared["solved"], preferred_element_type=jnp.float32).astype(jnp.bfloat16)
            for rows in (first, second)
        )
        n = sizes[k]
        come = lax.ppermute(sent, "col", swap)
        s["own"] = mine[:n] + come[:n]
        s["rest"] = mine[n:] + come[n:]

    def rides(k):
        return k + LATER < count and sizes[k] <= 3 * sizes[k + LATER]

    def leaving(k):
        s, n = state[k], sizes[k]
        return s.pop("rest")[2 * n :] + s["from_middle"][n:]

    def move_in(s, k):
        if line:
            sent = s["rest"]
            if k >= LATER and rides(k - LATER):
                out = leaving(k - LATER)
                n = out.shape[0]
                sent = jnp.concatenate([jnp.where(at_end, sent[:n], out), sent[n:]], axis=0)
            flying[k] = lax.ppermute(sent, "col", ends)

    def land(s, k):
        if line:
            s["from_end"] = flying.pop(k)

    def move_across(s, k):
        if line:
            n = sizes[k]
            s["from_middle"] = lax.ppermute(s["rest"][: 2 * n] + s["from_end"][n:], "col", across)

    def move_out(s, k):
        if line and not rides(k):
            s["from_inner"] = lax.ppermute(leaving(k), "col", outward)

    def settle(s, k):
        n = sizes[k]
        own = s.pop("own")
        if line:
            here = s["from_end"][:n].astype(jnp.float32) + s["from_middle"][:n].astype(jnp.float32)
            there = state[k + LATER]["from_end"][:n] if rides(k) else s["from_inner"]
            update = own.astype(jnp.float32) + jnp.where(at_end, there.astype(jnp.float32), here)
        else:
            groups = [[2 * g + c for g in range(chips)] for c in range(2)]
            pair = jnp.concatenate([own, s["rest"]], axis=0)
            update = lax.psum_scatter(
                pair, "col", scatter_dimension=0, axis_index_groups=groups, tiled=True
            ).astype(jnp.float32)
        rows = lax.slice_in_dim(shared["out"], starts[k], starts[k] + n, axis=0)
        shared["out"] = lax.dynamic_update_slice(shared["out"], rows - update, (starts[k], 0))

    stages = {
        0: (pick,),
        1: (share,),
        2: (share_again,),
        3: (multiply,),
        4: (move_in,),
        6: (land, move_across),
        7: (move_out,),
    }
    LATER = 3
    shared = {"solved": solved, "out": separator_rows}
    flying = {}
    for turn in range(count + 9):
        shared, state = lax.optimization_barrier((shared, state))
        for k in reversed(range(count)):
            for stage in stages.get(turn - k, ()):
                stage(state[k], k)
            if turn - k == (9 if rides(k) else 8):
                settle(state[k], k)
    return shared["out"]


def solution(mesh):
    in_specs = (
        P(("row", "col"), None),
        P(("row", "col")),
        P(("row", "col")),
        P(("row", "col")),
        P("col", "row"),
        P(),
        P("col", None),
        P("col", "row"),
    )
    out_specs = P("col", "row")
    return jax.shard_map(
        per_device, mesh=mesh, in_specs=in_specs, out_specs=out_specs, check_vma=False
    )
```

time: 677 us -> 512 us (0.76); the launches traced: 674 us -> 502 us
  waiting for transfers between devices: 439 us -> 210 us
  starting transfers between devices: 9.62 us -> 101 us
  matrix products: 59.1 us -> 126 us
  local copies, waits for them, and re-layouts: 60.7 us -> 8.59 us
  other arithmetic: 92.6 us -> 54.9 us
  between operations: 13.5 us -> 1.65 us
    reduce_scatter x1 -> x0, waiting for transfers between devices: 326 us -> none  [per_device(): lax.psum_scatter(jnp.dot(panel_solved.T, solved, preferred_element_type=j...]
    ppermute x0 -> x67, waiting for transfers between devices: none -> 210 us  [the longest x9 67.7 us: share(): s['first_in'] = lax.ppermute(s['first'], 'row', along_x)]
    all_gather x1 -> x0, waiting for transfers between devices: 109 us -> none  [per_device(): gathered = lax.all_gather(local_columns, 'row', axis=1, tiled=True)]
    ppermute x0 -> x67, starting transfers between devices: none -> 96.2 us  [the longest x9 36.1 us: move_across(): lax.ppermute(s['rest'][:2 * n] + s['from_end'][n:], 'col', across)]
    dot_general x1 -> x28, matrix products: 43.1 us -> 116 us  [the longest x18 65.3 us: multiply(): jnp.dot(rows, shared['solved'], preferred_element_type=jnp.float32)]
    scatter-add x1 -> x0, other arithmetic: 61.4 us -> none  [per_device(): summed = child_update.astype(jnp.float32).at[index_back[:, 0, :].ravel(),...]
    gather x2 -> x1, local copies, waits for them, and re-layouts: 36.4 us -> 0.58 us  [per_device(): local_pores = jnp.take(local_pores, order[chip], axis=0)]
    add x0 -> x49, other arithmetic: none -> 27.9 us  [the longest x9 8.04 us: multiply(): s['own'] = mine[:n] + come[:n]]
  transfers between devices with their start and end apart: 4 -> 68, of which waited for: 3 -> 24; matrix products, arithmetic and copies ran while one was open for 5% -> 30% of each run, Pallas kernels for 0% -> 0%
where the time goes in v1:
time: 512 us; the launch traced here: 502 us
  waiting for transfers between devices  210 us (41%)
  matrix products  126 us (25%)
  starting transfers between devices  101 us (20%)
  other arithmetic  54.9 us (11%)
  local copies, waits for them, and re-layouts  8.59 us (2%)
    ppermute x9, waiting for transfers between devices, share(): s['first_in'] = lax.ppermute(s['first'], 'row', along_x)  67.7 us
    dot_general x18, matrix products, multiply(): jnp.dot(rows, shared['solved'], preferred_element_type=jnp.float32)  65.3 us
    ppermute x4, waiting for transfers between devices, move_out(): s['from_inner'] = lax.ppermute(leaving(k), 'col', outward)  63.7 us
    ppermute x9, waiting for transfers between devices, move_in(): flying[k] = lax.ppermute(sent, 'col', ends)  48.3 us
    dot_general x9, matrix products, pick(): lax.dot_general(onehot, shared['solved'], (((1,), (1,)), ((), ())), prefe...  37 us
    ppermute x9, starting transfers between devices, move_across(): lax.ppermute(s['rest'][:2 * n] + s['from_end'][n:], 'col', across)  36.1 us
    ppermute x9, waiting for transfers between devices, share(): s['second_in'] = lax.ppermute(s['second'], 'row', along_y)  25.6 us
    ppermute x9, starting transfers between devices, move_in(): flying[k] = lax.ppermute(sent, 'col', ends)  17.8 us
  transfers between devices with their start and end apart: 68, of which 24 were waited for; matrix products, arithmetic and copies ran while one was open for 30% of the time, Pallas kernels for 0%

profile of v1, /device:TPU:0, one launch (start us, length us, event | category | flops | bytes accessed | tf_op | source)
XLA Modules:
  0.0 502.4 jit_solution(14079583530210277606)
XLA Ops:
  2.1 5.2 %all-to-all-start = ((f32[4,2,128]{2,1,0:T(2,128)}), f32[4,2,128]{2,1,0:T(2,128)S(1)}, u32[]{:S(2)}, u32[]{:S(2)}) async-start(f32[4,2,128]{2,1,0:T(2,128)} %pad_maximum_fusion.5), calls=%async_computation | async-start | bytes 8192 | tf_op jit(solution)/shard_map/all_to_all | solution.py:24
  12.0 13.8 %add_convert_fusion.7 = bf16[896,4096]{1,0:T(8,128)(2,1)S(1)} fusion(bf16[896,4096]{1,0:T(8,128)(2,1)} %param.13, s32[1024]{0:T(1024)S(1)} %pad_add_fusion.1, s32[1024]{0:T(1024)S(1)} %pad_add_fusion, bf16[1024]{0:T(1024)(128)(2,1)S(1)} %pad_maximum_fusion.6), kind=kOutput, calls=%fused_computation.3.clone.clone.clone.clone.1 | convolution fusion | flops 7533232128 | bytes 14690304 | tf_op jit(solution)/shard_map/dot_general | solution.py:40
  25.9 9.6 %convert_bitcast_fusion = bf16[896,4096]{0,1:T(8,128)(2,1)S(1)} fusion(bf16[896,896]{1,0:T(8,128)(2,1)S(1)} %copy-done, bf16[896,4096]{1,0:T(8,128)(2,1)S(1)} %add_convert_fusion.7), kind=kOutput, calls=%fused_computation.14 | convolution fusion | flops 6580338688 | bytes 16285696 | tf_op jit(solution)/shard_map/dot_general | solution.py:75
  35.4 2.4 fusion.33
  37.9 1.8 collective-permute-start
  41.2 3.5 fusion.31
  50.6 3.5 fusion.30
  56.5 4.1 collective-permute-done.4
  60.7 2.4 convolution_convert_fusion.14
  67.5 4.8 fusion.28
  72.4 2.5 convolution_convert_fusion.15
  75.7 5.9 %collective-permute-done.9 = bf16[192,896]{1,0:T(8,128)(2,1)S(1)} collective-permute-done((bf16[192,896]{1,0:T(8,128)(2,1)S(1)}, bf16[192,896]{1,0:T(8,128)(2,1)S(1)}, u32[]{:S(2)}, u32[]{:S(2)}) %collective-permute-start.9) | collective-permute-done | bytes 344096 | tf_op jit(solution)/shard_map/ppermute | solution.py:111
  81.6 2.6 convolution_convert_fusion.12
  88.6 5.6 %fusion.27 = bf16[640,896]{1,0:T(8,128)(2,1)S(1)} fusion(bf16[896,4096]{0,1:T(8,128)(2,1)S(1)} %convert_bitcast_fusion, s32[640]{0:T(1024)S(1)} %pad_add_fusion.2), kind=kOutput, calls=%fused_computation.66 | convolution fusion | flops 4700815360 | bytes 8489472 | tf_op jit(solution)/shard_map/dot_general | solution.py:103
  94.4 2.8 convolution_convert_fusion.13
  99.8 6.3 %collective-permute-done.14 = bf16[256,896]{1,0:T(8,128)(2,1)S(1)} collective-permute-done((bf16[256,896]{1,0:T(8,128)(2,1)S(1)}, bf16[256,896]{1,0:T(8,128)(2,1)S(1)}, u32[]{:S(2)}, u32[]{:S(2)}) %collective-permute-start.14) | collective-permute-done | bytes 458784 | tf_op jit(solution)/shard_map/ppermute | solution.py:111
  106.1 2.6 convolution_convert_fusion.10
  111.7 6.7 %fusion.25 = bf16[768,896]{1,0:T(8,128)(2,1)S(1)} fusion(bf16[896,4096]{0,1:T(8,128)(2,1)S(1)} %convert_bitcast_fusion, s32[768]{0:T(1024)S(1)} %pad_add_fusion.3), kind=kOutput, calls=%fused_computation.60 | convolution fusion | flops 5640978432 | bytes 8719360 | tf_op jit(solution)/shard_map/dot_general | solution.py:103
  118.5 2.6 convolution_convert_fusion.11
  125.2 9.4 %collective-permute-done.19 = bf16[320,896]{1,0:T(8,128)(2,1)S(1)} collective-permute-done((bf16[320,896]{1,0:T(8,128)(2,1)S(1)}, bf16[320,896]{1,0:T(8,128)(2,1)S(1)}, u32[]{:S(2)}, u32[]{:S(2)}) %collective-permute-start.19) | collective-permute-done | bytes 573472 | tf_op jit(solution)/shard_map/ppermute | solution.py:111
  136.9 3.7 convolution_convert_fusion.6
  143.2 5.6 %fusion.26 = bf16[640,896]{1,0:T(8,128)(2,1)S(1)} fusion(bf16[896,4096]{0,1:T(8,128)(2,1)S(1)} %convert_bitcast_fusion, s32[640]{0:T(1024)S(1)} %pad_add_fusion.4), kind=kOutput, calls=%fused_computation.65 | convolution fusion | flops 4700815360 | bytes 8489472 | tf_op jit(solution)/shard_map/dot_general | solution.py:103
  148.9 2.4 convolution_convert_fusion.7
  154.5 2.2 collective-permute-done.24
  156.7 4.4 collective-permute-start.35
  161.1 11.4 %collective-permute-done.26 = bf16[384,896]{1,0:T(8,128)(2,1)S(1)} collective-permute-done((bf16[384,896]{1,0:T(8,128)(2,1)S(1)}, bf16[384,896]{1,0:T(8,128)(2,1)S(1)}, u32[]{:S(2)}, u32[]{:S(2)}) %collective-permute-start.26) | collective-permute-done | bytes 688160 | tf_op jit(solution)/shard_map/ppermute | solution.py:111
  173.6 1.8 collective-permute-start.29
  175.5 4.3 convolution_convert_fusion.4
  182.1 3.5 fusion.29
  188.3 3.2 convolution_convert_fusion.5
  193.3 18.1 %collective-permute-done.33 = bf16[320,896]{1,0:T(8,128)(2,1)S(1)} collective-permute-done((bf16[320,896]{1,0:T(8,128)(2,1)S(1)}, bf16[320,896]{1,0:T(8,128)(2,1)S(1)}, u32[]{:S(2)}, u32[]{:S(2)}) %collective-permute-start.33) | collective-permute-done | bytes 573472 | tf_op jit(solution)/shard_map/ppermute | solution.py:111
  213.8 11.9 %collective-permute-done.34 = bf16[320,896]{1,0:T(8,128)(2,1)S(1)} collective-permute-done((bf16[320,896]{1,0:T(8,128)(2,1)S(1)}, bf16[320,896]{1,0:T(8,128)(2,1)S(1)}, u32[]{:S(2)}, u32[]{:S(2)}) %collective-permute-start.34) | collective-permute-done | bytes 573472 | tf_op jit(solution)/shard_map/ppermute | solution.py:112
  225.7 5.2 %collective-permute-start.42 = (bf16[192,4096]{1,0:T(8,128)(2,1)}, bf16[192,4096]{1,0:T(8,128)(2,1)}, u32[]{:S(2)}, u32[]{:S(2)}) collective-permute-start(bf16[192,4096]{1,0:T(8,128)(2,1)} %pad_maximum_fusion.3), channel_id=1, source_target_pairs={{0,2},{1,3},{2,0},{3,1},{4,6},{5,7},{6,4},{7,5},{8,10},{9,11},{10,... | collective-permute-start | bytes 4718600 | tf_op jit(solution)/shard_map/ppermute | solution.py:152
  230.9 6.2 %convolution_convert_fusion = bf16[384,4096]{1,0:T(8,128)(2,1)} fusion(bf16[896,4096]{0,1:T(8,128)(2,1)S(1)} %convert_bitcast_fusion, bf16[384,896]{1,0:T(8,128)(2,1)} %add.359, bf16[384,896]{1,0:T(8,128)(2,1)} %collective-permute-done.31), kind=kOutput, calls=%fused_computation.22 | convolution fusion | flops 2820489216 | bytes 11862016 | tf_op jit(solution)/shard_map/dot_general | solution.py:130
  238.2 7.6 %collective-permute-start.36 = (bf16[96,4096]{1,0:T(8,128)(2,1)}, bf16[96,4096]{1,0:T(8,128)(2,1)}, u32[]{:S(2)}, u32[]{:S(2)}) collective-permute-start(bf16[96,4096]{1,0:T(8,128)(2,1)} %slice_add_fusion.13), channel_id=1, source_target_pairs={{0,0},{1,1},{2,4},{3,5},{4,2},{5,3},{6,6},{7,7},{8,8},{9,9},{10,12... | collective-permute-start | bytes 2359304 | tf_op jit(solution)/shard_map/ppermute | solution.py:161
  254.5 4.9 convolution_convert_fusion.1
  261.2 10.7 %collective-permute-done.40 = bf16[192,896]{1,0:T(8,128)(2,1)S(1)} collective-permute-done((bf16[192,896]{1,0:T(8,128)(2,1)S(1)}, bf16[192,896]{1,0:T(8,128)(2,1)S(1)}, u32[]{:S(2)}, u32[]{:S(2)}) %collective-permute-start.40) | collective-permute-done | bytes 344096 | tf_op jit(solution)/shard_map/ppermute | solution.py:111
  272.5 8.8 %collective-permute-done.41 = bf16[192,896]{1,0:T(8,128)(2,1)S(1)} collective-permute-done((bf16[192,896]{1,0:T(8,128)(2,1)S(1)}, bf16[192,896]{1,0:T(8,128)(2,1)S(1)}, u32[]{:S(2)}, u32[]{:S(2)}) %collective-permute-start.41) | collective-permute-done | bytes 344096 | tf_op jit(solution)/shard_map/ppermute | solution.py:112
  281.3 2.3 slice_add_fusion.10
  283.7 9.5 %collective-permute-start.43 = (bf16[128,4096]{1,0:T(8,128)(2,1)}, bf16[128,4096]{1,0:T(8,128)(2,1)}, u32[]{:S(2)}, u32[]{:S(2)}) collective-permute-start(bf16[128,4096]{1,0:T(8,128)(2,1)} %slice_add_fusion.10), channel_id=1, source_target_pairs={{0,0},{1,1},{2,4},{3,5},{4,2},{5,3},{6,6},{7,7},{8,8},{9,9},{10,12... | collective-permute-start | bytes 3145736 | tf_op jit(solution)/shard_map/ppermute | solution.py:161
  293.1 5.5 %convolution_convert_fusion.2 = bf16[320,4096]{1,0:T(8,128)(2,1)} fusion(bf16[896,4096]{0,1:T(8,128)(2,1)S(1)} %convert_bitcast_fusion, bf16[320,896]{1,0:T(8,128)(2,1)} %add.366, bf16[320,896]{1,0:T(8,128)(2,1)} %collective-permute-done.38), kind=kOutput, calls=%fused_computation.24 | convolution fusion | flops 2350407680 | bytes 11108352 | tf_op jit(solution)/shard_map/dot_general | solution.py:130
  304.4 5.7 %convolution_convert_fusion.3 = bf16[320,4096]{1,0:T(8,128)(2,1)} fusion(bf16[896,4096]{0,1:T(8,128)(2,1)S(1)} %convert_bitcast_fusion, bf16[320,896]{1,0:T(8,128)(2,1)} %add.367, bf16[320,896]{1,0:T(8,128)(2,1)} %collective-permute-done.39), kind=kOutput, calls=%fused_computation.25 | convolution fusion | flops 2350407680 | bytes 11108352 | tf_op jit(solution)/shard_map/dot_general | solution.py:130
  314.8 1.8 collective-permute-done.47
  319.3 2.4 collective-permute-done.48
  321.6 4.9 collective-permute-done.49
  326.6 2.6 slice_add_fusion.6
  329.2 11.6 %collective-permute-start.50 = (bf16[160,4096]{1,0:T(8,128)(2,1)}, bf16[160,4096]{1,0:T(8,128)(2,1)}, u32[]{:S(2)}, u32[]{:S(2)}) collective-permute-start(bf16[160,4096]{1,0:T(8,128)(2,1)} %slice_add_fusion.6), channel_id=1, source_target_pairs={{0,0},{1,1},{2,4},{3,5},{4,2},{5,3},{6,6},{7,7},{8,8},{9,9},{10,12... | collective-permute-start | bytes 3932168 | tf_op jit(solution)/shard_map/ppermute | solution.py:161
  340.8 4.9 convolution_convert_fusion.8
  348.0 3.7 convolution_convert_fusion.9
  352.7 1.8 subtract_dynamic-update-slice_fusion.5
  357.4 1.8 slice_add_fusion.23
  359.2 17.8 %collective-permute-done.54 = bf16[288,4096]{1,0:T(8,128)(2,1)S(1)} collective-permute-done((bf16[288,4096]{1,0:T(8,128)(2,1)}, bf16[288,4096]{1,0:T(8,128)(2,1)S(1)}, u32[]{:S(2)}, u32[]{:S(2)}) %collective-permute-start.54) | collective-permute-done | bytes 2359328 | tf_op jit(solution)/shard_map/ppermute | solution.py:152
  378.4 2.1 collective-permute-start.55
  380.4 3.1 convolution_convert_fusion.16
  386.0 1.7 collective-permute-start.60
  389.4 2.3 convolution_convert_fusion.17
  393.7 25.5 %collective-permute-done.57 = bf16[240,4096]{1,0:T(8,128)(2,1)S(1)} collective-permute-done((bf16[240,4096]{1,0:T(8,128)(2,1)}, bf16[240,4096]{1,0:T(8,128)(2,1)S(1)}, u32[]{:S(2)}, u32[]{:S(2)}) %collective-permute-start.57) | collective-permute-done | bytes 1966112 | tf_op jit(solution)/shard_map/ppermute | solution.py:152
  421.5 3.2 collective-permute-start.64
  424.6 1.8 subtract_dynamic-update-slice_fusion.2
  426.4 34.9 %collective-permute-done.58 = bf16[96,4096]{1,0:T(8,128)(2,1)S(1)} collective-permute-done((bf16[96,4096]{1,0:T(8,128)(2,1)S(1)}, bf16[96,4096]{1,0:T(8,128)(2,1)S(1)}, u32[]{:S(2)}, u32[]{:S(2)}) %collective-permute-start.58) | collective-permute-done | bytes 786464 | tf_op jit(solution)/shard_map/ppermute | solution.py:165
  464.6 2.0 fusion.32
  466.6 15.4 %collective-permute-done.61 = bf16[80,4096]{1,0:T(8,128)(2,1)S(1)} collective-permute-done((bf16[80,4096]{1,0:T(8,128)(2,1)S(1)}, bf16[80,4096]{1,0:T(8,128)(2,1)S(1)}, u32[]{:S(2)}, u32[]{:S(2)}) %collective-permute-start.61) | collective-permute-done | bytes 655392 | tf_op jit(solution)/shard_map/ppermute | solution.py:165
  485.0 8.3 %collective-permute-done.63 = bf16[48,4096]{1,0:T(8,128)(2,1)S(1)} collective-permute-done((bf16[48,4096]{1,0:T(8,128)(2,1)S(1)}, bf16[48,4096]{1,0:T(8,128)(2,1)S(1)}, u32[]{:S(2)}, u32[]{:S(2)}) %collective-permute-start.63) | collective-permute-done | bytes 393248 | tf_op jit(solution)/shard_map/ppermute | solution.py:165
  495.1 5.1 %collective-permute-done.66 = bf16[16,4096]{1,0:T(8,128)(2,1)S(1)} collective-permute-done((bf16[16,4096]{1,0:T(8,128)(2,1)S(1)}, bf16[16,4096]{1,0:T(8,128)(2,1)S(1)}, u32[]{:S(2)}, u32[]{:S(2)}) %collective-permute-start.66) | collective-permute-done | bytes 131104 | tf_op jit(solution)/shard_map/ppermute | solution.py:165
  (326 shorter events, 105.1 us)
Async XLA Ops:
  2.1 9.8 %all-to-all-start = ((f32[4,2,128]{2,1,0:T(2,128)}), f32[4,2,128]{2,1,0:T(2,128)S(1)}, u32[]{:S(2)}, u32[]{:S(2)}) async-start(f32[4,2,128]{2,1,0:T(2,128)} %pad_maximum_fusion.5), calls=%async_computation | async-start | bytes 8192 | tf_op jit(solution)/shard_map/all_to_all | solution.py:24
  37.9 6.9 %collective-permute-start = (bf16[128,896]{1,0:T(8,128)(2,1)S(1)}, bf16[128,896]{1,0:T(8,128)(2,1)S(1)}, u32[]{:S(2)}, u32[]{:S(2)}) collective-permute-start(bf16[128,896]{1,0:T(8,128)(2,1)S(1)} %get-tuple-element.269), channel_id=1, source_target_pairs={{0,8},{8,0},{16,24},{24,16},{1,9},{9,1},{17,25},{25,17},{2,10},{10... | collective-permute-start | bytes 688136 | tf_op jit(solution)/shard_map/ppermute | solution.py:111
  46.3 8.5 %collective-permute-start.2 = (bf16[128,896]{1,0:T(8,128)(2,1)S(1)}, bf16[128,896]{1,0:T(8,128)(2,1)S(1)}, u32[]{:S(2)}, u32[]{:S(2)}) collective-permute-start(bf16[128,896]{1,0:T(8,128)(2,1)S(1)} %add.327), channel_id=1, source_target_pairs={{0,16},{8,24},{16,0},{24,8},{1,17},{9,25},{17,1},{25,9},{2,18},{10... | collective-permute-start | bytes 688136 | tf_op jit(solution)/shard_map/ppermute | solution.py:121
  47.9 8.6 %collective-permute-start.3 = (bf16[128,896]{1,0:T(8,128)(2,1)S(1)}, bf16[128,896]{1,0:T(8,128)(2,1)S(1)}, u32[]{:S(2)}, u32[]{:S(2)}) collective-permute-start(bf16[128,896]{1,0:T(8,128)(2,1)S(1)} %add.328), channel_id=1, source_target_pairs={{0,8},{8,0},{16,24},{24,16},{1,9},{9,1},{17,25},{25,17},{2,10},{10... | collective-permute-start | bytes 688136 | tf_op jit(solution)/shard_map/ppermute | solution.py:122
  48.5 12.1 %collective-permute-start.4 = (bf16[192,896]{1,0:T(8,128)(2,1)S(1)}, bf16[192,896]{1,0:T(8,128)(2,1)S(1)}, u32[]{:S(2)}, u32[]{:S(2)}) collective-permute-start(bf16[192,896]{1,0:T(8,128)(2,1)S(1)} %get-tuple-element.281), channel_id=1, source_target_pairs={{0,8},{8,0},{16,24},{24,16},{1,9},{9,1},{17,25},{25,17},{2,10},{10... | collective-permute-start | bytes 1032200 | tf_op jit(solution)/shard_map/ppermute | solution.py:111
  50.0 10.6 %collective-permute-start.5 = (bf16[192,896]{1,0:T(8,128)(2,1)S(1)}, bf16[192,896]{1,0:T(8,128)(2,1)S(1)}, u32[]{:S(2)}, u32[]{:S(2)}) collective-permute-start(bf16[192,896]{1,0:T(8,128)(2,1)S(1)} %get-tuple-element.283), channel_id=1, source_target_pairs={{0,16},{8,24},{16,0},{24,8},{1,17},{9,25},{17,1},{25,9},{2,18},{10... | collective-permute-start | bytes 1032200 | tf_op jit(solution)/shard_map/ppermute | solution.py:112
  63.1 11.8 %collective-permute-start.6 = (bf16[128,4096]{1,0:T(8,128)(2,1)S(1)}, bf16[128,4096]{1,0:T(8,128)(2,1)S(1)}, u32[]{:S(2)}, u32[]{:S(2)}) collective-permute-start(bf16[128,4096]{1,0:T(8,128)(2,1)S(1)} %convolution_convert_fusion.14), channel_id=1, source_target_pairs={{0,1},{1,0},{2,3},{3,2},{4,5},{5,4},{6,7},{7,6},{8,9},{9,8},{10,11... | collective-permute-start | bytes 3145736 | tf_op jit(solution)/shard_map/ppermute | solution.py:134
  63.3 12.4 %collective-permute-start.7 = (bf16[192,896]{1,0:T(8,128)(2,1)S(1)}, bf16[192,896]{1,0:T(8,128)(2,1)S(1)}, u32[]{:S(2)}, u32[]{:S(2)}) collective-permute-start(bf16[192,896]{1,0:T(8,128)(2,1)S(1)} %add.333), channel_id=1, source_target_pairs={{0,16},{8,24},{16,0},{24,8},{1,17},{9,25},{17,1},{25,9},{2,18},{10... | collective-permute-start | bytes 1032200 | tf_op jit(solution)/shard_map/ppermute | solution.py:121
  64.0 11.7 %collective-permute-start.8 = (bf16[192,896]{1,0:T(8,128)(2,1)S(1)}, bf16[192,896]{1,0:T(8,128)(2,1)S(1)}, u32[]{:S(2)}, u32[]{:S(2)}) collective-permute-start(bf16[192,896]{1,0:T(8,128)(2,1)S(1)} %add.334), channel_id=1, source_target_pairs={{0,8},{8,0},{16,24},{24,16},{1,9},{9,1},{17,25},{25,17},{2,10},{10... | collective-permute-start | bytes 1032200 | tf_op jit(solution)/shard_map/ppermute | solution.py:122
  64.6 17.0 %collective-permute-start.9 = (bf16[192,896]{1,0:T(8,128)(2,1)S(1)}, bf16[192,896]{1,0:T(8,128)(2,1)S(1)}, u32[]{:S(2)}, u32[]{:S(2)}) collective-permute-start(bf16[192,896]{1,0:T(8,128)(2,1)S(1)} %get-tuple-element.295), channel_id=1, source_target_pairs={{0,8},{8,0},{16,24},{24,16},{1,9},{9,1},{17,25},{25,17},{2,10},{10... | collective-permute-start | bytes 1032200 | tf_op jit(solution)/shard_map/ppermute | solution.py:111
  66.1 15.5 %collective-permute-start.10 = (bf16[192,896]{1,0:T(8,128)(2,1)S(1)}, bf16[192,896]{1,0:T(8,128)(2,1)S(1)}, u32[]{:S(2)}, u32[]{:S(2)}) collective-permute-start(bf16[192,896]{1,0:T(8,128)(2,1)S(1)} %get-tuple-element.297), channel_id=1, source_target_pairs={{0,16},{8,24},{16,0},{24,8},{1,17},{9,25},{17,1},{25,9},{2,18},{10... | collective-permute-start | bytes 1032200 | tf_op jit(solution)/shard_map/ppermute | solution.py:112
  84.2 13.0 %collective-permute-start.11 = (bf16[192,4096]{1,0:T(8,128)(2,1)S(1)}, bf16[192,4096]{1,0:T(8,128)(2,1)S(1)}, u32[]{:S(2)}, u32[]{:S(2)}) collective-permute-start(bf16[192,4096]{1,0:T(8,128)(2,1)S(1)} %convolution_convert_fusion.12), channel_id=1, source_target_pairs={{0,1},{1,0},{2,3},{3,2},{4,5},{5,4},{6,7},{7,6},{8,9},{9,8},{10,11... | collective-permute-start | bytes 4718600 | tf_op jit(solution)/shard_map/ppermute | solution.py:134
  84.4 15.4 %collective-permute-start.12 = (bf16[192,896]{1,0:T(8,128)(2,1)S(1)}, bf16[192,896]{1,0:T(8,128)(2,1)S(1)}, u32[]{:S(2)}, u32[]{:S(2)}) collective-permute-start(bf16[192,896]{1,0:T(8,128)(2,1)S(1)} %add.339), channel_id=1, source_target_pairs={{0,16},{8,24},{16,0},{24,8},{1,17},{9,25},{17,1},{25,9},{2,18},{10... | collective-permute-start | bytes 1032200 | tf_op jit(solution)/shard_map/ppermute | solution.py:121
  86.0 13.8 %collective-permute-start.13 = (bf16[192,896]{1,0:T(8,128)(2,1)S(1)}, bf16[192,896]{1,0:T(8,128)(2,1)S(1)}, u32[]{:S(2)}, u32[]{:S(2)}) collective-permute-start(bf16[192,896]{1,0:T(8,128)(2,1)S(1)} %add.340), channel_id=1, source_target_pairs={{0,8},{8,0},{16,24},{24,16},{1,9},{9,1},{17,25},{25,17},{2,10},{10... | collective-permute-start | bytes 1032200 | tf_op jit(solution)/shard_map/ppermute | solution.py:122
  86.6 19.4 %collective-permute-start.14 = (bf16[256,896]{1,0:T(8,128)(2,1)S(1)}, bf16[256,896]{1,0:T(8,128)(2,1)S(1)}, u32[]{:S(2)}, u32[]{:S(2)}) collective-permute-start(bf16[256,896]{1,0:T(8,128)(2,1)S(1)} %get-tuple-element.311), channel_id=1, source_target_pairs={{0,8},{8,0},{16,24},{24,16},{1,9},{9,1},{17,25},{25,17},{2,10},{10... | collective-permute-start | bytes 1376264 | tf_op jit(solution)/shard_map/ppermute | solution.py:111
  88.1 18.0 %collective-permute-start.15 = (bf16[256,896]{1,0:T(8,128)(2,1)S(1)}, bf16[256,896]{1,0:T(8,128)(2,1)S(1)}, u32[]{:S(2)}, u32[]{:S(2)}) collective-permute-start(bf16[256,896]{1,0:T(8,128)(2,1)S(1)} %get-tuple-element.313), channel_id=1, source_target_pairs={{0,16},{8,24},{16,0},{24,8},{1,17},{9,25},{17,1},{25,9},{2,18},{10... | collective-permute-start | bytes 1376264 | tf_op jit(solution)/shard_map/ppermute | solution.py:112
  97.2 38.6 %collective-permute-start.21 = (bf16[96,4096]{1,0:T(8,128)(2,1)S(1)}, bf16[96,4096]{1,0:T(8,128)(2,1)S(1)}, u32[]{:S(2)}, u32[]{:S(2)}) collective-permute-start(bf16[96,4096]{1,0:T(8,128)(2,1)S(1)} %slice_add_fusion.15), channel_id=1, source_target_pairs={{0,2},{1,3},{2,0},{3,1},{4,6},{5,7},{6,4},{7,5},{8,10},{9,11},{10,... | collective-permute-start | bytes 2359304 | tf_op jit(solution)/shard_map/ppermute | solution.py:152
  108.7 12.5 %collective-permute-start.16 = (bf16[192,4096]{1,0:T(8,128)(2,1)S(1)}, bf16[192,4096]{1,0:T(8,128)(2,1)S(1)}, u32[]{:S(2)}, u32[]{:S(2)}) collective-permute-start(bf16[192,4096]{1,0:T(8,128)(2,1)S(1)} %convolution_convert_fusion.10), channel_id=1, source_target_pairs={{0,1},{1,0},{2,3},{3,2},{4,5},{5,4},{6,7},{7,6},{8,9},{9,8},{10,11... | collective-permute-start | bytes 4718600 | tf_op jit(solution)/shard_map/ppermute | solution.py:134
  108.9 14.7 %collective-permute-start.17 = (bf16[256,896]{1,0:T(8,128)(2,1)S(1)}, bf16[256,896]{1,0:T(8,128)(2,1)S(1)}, u32[]{:S(2)}, u32[]{:S(2)}) collective-permute-start(bf16[256,896]{1,0:T(8,128)(2,1)S(1)} %add.345), channel_id=1, source_target_pairs={{0,16},{8,24},{16,0},{24,8},{1,17},{9,25},{17,1},{25,9},{2,18},{10... | collective-permute-start | bytes 1376264 | tf_op jit(solution)/shard_map/ppermute | solution.py:121
  109.6 15.6 %collective-permute-start.18 = (bf16[256,896]{1,0:T(8,128)(2,1)S(1)}, bf16[256,896]{1,0:T(8,128)(2,1)S(1)}, u32[]{:S(2)}, u32[]{:S(2)}) collective-permute-start(bf16[256,896]{1,0:T(8,128)(2,1)S(1)} %add.346), channel_id=1, source_target_pairs={{0,8},{8,0},{16,24},{24,16},{1,9},{9,1},{17,25},{25,17},{2,10},{10... | collective-permute-start | bytes 1376264 | tf_op jit(solution)/shard_map/ppermute | solution.py:122
  110.2 24.4 %collective-permute-start.19 = (bf16[320,896]{1,0:T(8,128)(2,1)S(1)}, bf16[320,896]{1,0:T(8,128)(2,1)S(1)}, u32[]{:S(2)}, u32[]{:S(2)}) collective-permute-start(bf16[320,896]{1,0:T(8,128)(2,1)S(1)} %get-tuple-element.329), channel_id=1, source_target_pairs={{0,8},{8,0},{16,24},{24,16},{1,9},{9,1},{17,25},{25,17},{2,10},{10... | collective-permute-start | bytes 1720328 | tf_op jit(solution)/shard_map/ppermute | solution.py:111
  121.2 14.6 %collective-permute-start.20 = (bf16[320,896]{1,0:T(8,128)(2,1)S(1)}, bf16[320,896]{1,0:T(8,128)(2,1)S(1)}, u32[]{:S(2)}, u32[]{:S(2)}) collective-permute-start(bf16[320,896]{1,0:T(8,128)(2,1)S(1)} %get-tuple-element.331), channel_id=1, source_target_pairs={{0,16},{8,24},{16,0},{24,8},{1,17},{9,25},{17,1},{25,9},{2,18},{10... | collective-permute-start | bytes 1720328 | tf_op jit(solution)/shard_map/ppermute | solution.py:112
  123.6 49.9 %collective-permute-start.28 = (bf16[144,4096]{1,0:T(8,128)(2,1)S(1)}, bf16[144,4096]{1,0:T(8,128)(2,1)S(1)}, u32[]{:S(2)}, u32[]{:S(2)}) collective-permute-start(bf16[144,4096]{1,0:T(8,128)(2,1)S(1)} %slice_add_fusion.9), channel_id=1, source_target_pairs={{0,2},{1,3},{2,0},{3,1},{4,6},{5,7},{6,4},{7,5},{8,10},{9,11},{10,... | collective-permute-start | bytes 3538952 | tf_op jit(solution)/shard_map/ppermute | solution.py:152
  135.8 17.2 %collective-permute-start.22 = (bf16[64,4096]{1,0:T(8,128)(2,1)S(1)}, bf16[64,4096]{1,0:T(8,128)(2,1)S(1)}, u32[]{:S(2)}, u32[]{:S(2)}) collective-permute-start(bf16[64,4096]{1,0:T(8,128)(2,1)S(1)} %slice_add_fusion.21), channel_id=1, source_target_pairs={{0,0},{1,1},{2,4},{3,5},{4,2},{5,3},{6,6},{7,7},{8,8},{9,9},{10,12... | collective-permute-start | bytes 1572872 | tf_op jit(solution)/shard_map/ppermute | solution.py:161
  140.7 10.6 %collective-permute-start.23 = (bf16[256,4096]{1,0:T(8,128)(2,1)}, bf16[256,4096]{1,0:T(8,128)(2,1)S(1)}, u32[]{:S(2)}, u32[]{:S(2)}) collective-permute-start(bf16[256,4096]{1,0:T(8,128)(2,1)} %convolution_convert_fusion.6), channel_id=1, source_target_pairs={{0,1},{1,0},{2,3},{3,2},{4,5},{5,4},{6,7},{7,6},{8,9},{9,8},{10,11... | collective-permute-start | bytes 6291464 | tf_op jit(solution)/shard_map/ppermute | solution.py:134
  140.8 15.8 %collective-permute-start.24 = (bf16[320,896]{1,0:T(8,128)(2,1)S(1)}, bf16[320,896]{1,0:T(8,128)(2,1)S(1)}, u32[]{:S(2)}, u32[]{:S(2)}) collective-permute-start(bf16[320,896]{1,0:T(8,128)(2,1)S(1)} %add.352), channel_id=1, source_target_pairs={{0,16},{8,24},{16,0},{24,8},{1,17},{9,25},{17,1},{25,9},{2,18},{10... | collective-permute-start | bytes 1720328 | tf_op jit(solution)/shard_map/ppermute | solution.py:121
  142.5 18.6 %collective-permute-start.25 = (bf16[320,896]{1,0:T(8,128)(2,1)S(1)}, bf16[320,896]{1,0:T(8,128)(2,1)S(1)}, u32[]{:S(2)}, u32[]{:S(2)}) collective-permute-start(bf16[320,896]{1,0:T(8,128)(2,1)S(1)} %add.353), channel_id=1, source_target_pairs={{0,8},{8,0},{16,24},{24,16},{1,9},{9,1},{17,25},{25,17},{2,10},{10... | collective-permute-start | bytes 1720328 | tf_op jit(solution)/shard_map/ppermute | solution.py:122
  151.3 21.1 %collective-permute-start.26 = (bf16[384,896]{1,0:T(8,128)(2,1)S(1)}, bf16[384,896]{1,0:T(8,128)(2,1)S(1)}, u32[]{:S(2)}, u32[]{:S(2)}) collective-permute-start(bf16[384,896]{1,0:T(8,128)(2,1)S(1)} %get-tuple-element.350), channel_id=1, source_target_pairs={{0,8},{8,0},{16,24},{24,16},{1,9},{9,1},{17,25},{25,17},{2,10},{10... | collective-permute-start | bytes 2064392 | tf_op jit(solution)/shard_map/ppermute | solution.py:111
  153.0 19.4 %collective-permute-start.27 = (bf16[384,896]{1,0:T(8,128)(2,1)S(1)}, bf16[384,896]{1,0:T(8,128)(2,1)S(1)}, u32[]{:S(2)}, u32[]{:S(2)}) collective-permute-start(bf16[384,896]{1,0:T(8,128)(2,1)S(1)} %get-tuple-element.352), channel_id=1, source_target_pairs={{0,16},{8,24},{16,0},{24,8},{1,17},{9,25},{17,1},{25,9},{2,18},{10... | collective-permute-start | bytes 2064392 | tf_op jit(solution)/shard_map/ppermute | solution.py:112
  156.7 80.4 %collective-permute-start.35 = (bf16[144,4096]{1,0:T(8,128)(2,1)S(1)}, bf16[144,4096]{1,0:T(8,128)(2,1)S(1)}, u32[]{:S(2)}, u32[]{:S(2)}) collective-permute-start(bf16[144,4096]{1,0:T(8,128)(2,1)S(1)} %slice_add_fusion.8), channel_id=1, source_target_pairs={{0,2},{1,3},{2,0},{3,1},{4,6},{5,7},{6,4},{7,5},{8,10},{9,11},{10,... | collective-permute-start | bytes 3538952 | tf_op jit(solution)/shard_map/ppermute | solution.py:152
  173.6 57.3 %collective-permute-start.29 = (bf16[96,4096]{1,0:T(8,128)(2,1)S(1)}, bf16[96,4096]{1,0:T(8,128)(2,1)}, u32[]{:S(2)}, u32[]{:S(2)}) collective-permute-start(bf16[96,4096]{1,0:T(8,128)(2,1)S(1)} %slice_add_fusion.14), channel_id=1, source_target_pairs={{0,0},{1,1},{2,4},{3,5},{4,2},{5,3},{6,6},{7,7},{8,8},{9,9},{10,12... | collective-permute-start | bytes 2359304 | tf_op jit(solution)/shard_map/ppermute | solution.py:161
  179.8 11.7 %collective-permute-start.30 = (bf16[320,4096]{1,0:T(8,128)(2,1)}, bf16[320,4096]{1,0:T(8,128)(2,1)S(1)}, u32[]{:S(2)}, u32[]{:S(2)}) collective-permute-start(bf16[320,4096]{1,0:T(8,128)(2,1)} %convolution_convert_fusion.4), channel_id=1, source_target_pairs={{0,1},{1,0},{2,3},{3,2},{4,5},{5,4},{6,7},{7,6},{8,9},{9,8},{10,11... | collective-permute-start | bytes 7864328 | tf_op jit(solution)/shard_map/ppermute | solution.py:134
  180.8 50.1 %collective-permute-start.31 = (bf16[384,896]{1,0:T(8,128)(2,1)}, bf16[384,896]{1,0:T(8,128)(2,1)}, u32[]{:S(2)}, u32[]{:S(2)}) collective-permute-start(bf16[384,896]{1,0:T(8,128)(2,1)} %add.359), channel_id=1, source_target_pairs={{0,16},{8,24},{16,0},{24,8},{1,17},{9,25},{17,1},{25,9},{2,18},{10... | collective-permute-start | bytes 2064392 | tf_op jit(solution)/shard_map/ppermute | solution.py:121
  181.5 49.4 %collective-permute-start.32 = (bf16[384,896]{1,0:T(8,128)(2,1)S(1)}, bf16[384,896]{1,0:T(8,128)(2,1)}, u32[]{:S(2)}, u32[]{:S(2)}) collective-permute-start(bf16[384,896]{1,0:T(8,128)(2,1)S(1)} %add.360), channel_id=1, source_target_pairs={{0,8},{8,0},{16,24},{24,16},{1,9},{9,1},{17,25},{25,17},{2,10},{10... | collective-permute-start | bytes 2064392 | tf_op jit(solution)/shard_map/ppermute | solution.py:122
  191.5 19.9 %collective-permute-start.33 = (bf16[320,896]{1,0:T(8,128)(2,1)S(1)}, bf16[320,896]{1,0:T(8,128)(2,1)S(1)}, u32[]{:S(2)}, u32[]{:S(2)}) collective-permute-start(bf16[320,896]{1,0:T(8,128)(2,1)S(1)} %get-tuple-element.374), channel_id=1, source_target_pairs={{0,8},{8,0},{16,24},{24,16},{1,9},{9,1},{17,25},{25,17},{2,10},{10... | collective-permute-start | bytes 1720328 | tf_op jit(solution)/shard_map/ppermute | solution.py:111
  211.4 14.3 %collective-permute-start.34 = (bf16[320,896]{1,0:T(8,128)(2,1)S(1)}, bf16[320,896]{1,0:T(8,128)(2,1)S(1)}, u32[]{:S(2)}, u32[]{:S(2)}) collective-permute-start(bf16[320,896]{1,0:T(8,128)(2,1)S(1)} %get-tuple-element.376), channel_id=1, source_target_pairs={{0,16},{8,24},{16,0},{24,8},{1,17},{9,25},{17,1},{25,9},{2,18},{10... | collective-permute-start | bytes 1720328 | tf_op jit(solution)/shard_map/ppermute | solution.py:112
  225.7 55.6 %collective-permute-start.42 = (bf16[192,4096]{1,0:T(8,128)(2,1)}, bf16[192,4096]{1,0:T(8,128)(2,1)}, u32[]{:S(2)}, u32[]{:S(2)}) collective-permute-start(bf16[192,4096]{1,0:T(8,128)(2,1)} %pad_maximum_fusion.3), channel_id=1, source_target_pairs={{0,2},{1,3},{2,0},{3,1},{4,6},{5,7},{6,4},{7,5},{8,10},{9,11},{10,... | collective-permute-start | bytes 4718600 | tf_op jit(solution)/shard_map/ppermute | solution.py:152
  237.1 22.4 %collective-permute-start.37 = (bf16[384,4096]{1,0:T(8,128)(2,1)}, bf16[384,4096]{1,0:T(8,128)(2,1)S(1)}, u32[]{:S(2)}, u32[]{:S(2)}) collective-permute-start(bf16[384,4096]{1,0:T(8,128)(2,1)} %convolution_convert_fusion), channel_id=1, source_target_pairs={{0,1},{1,0},{2,3},{3,2},{4,5},{5,4},{6,7},{7,6},{8,9},{9,8},{10,11... | collective-permute-start | bytes 9437192 | tf_op jit(solution)/shard_map/ppermute | solution.py:134
  238.2 43.1 %collective-permute-start.36 = (bf16[96,4096]{1,0:T(8,128)(2,1)}, bf16[96,4096]{1,0:T(8,128)(2,1)}, u32[]{:S(2)}, u32[]{:S(2)}) collective-permute-start(bf16[96,4096]{1,0:T(8,128)(2,1)} %slice_add_fusion.13), channel_id=1, source_target_pairs={{0,0},{1,1},{2,4},{3,5},{4,2},{5,3},{6,6},{7,7},{8,8},{9,9},{10,12... | collective-permute-start | bytes 2359304 | tf_op jit(solution)/shard_map/ppermute | solution.py:161
  246.8 34.5 %collective-permute-start.38 = (bf16[320,896]{1,0:T(8,128)(2,1)}, bf16[320,896]{1,0:T(8,128)(2,1)}, u32[]{:S(2)}, u32[]{:S(2)}) collective-permute-start(bf16[320,896]{1,0:T(8,128)(2,1)} %add.366), channel_id=1, source_target_pairs={{0,16},{8,24},{16,0},{24,8},{1,17},{9,25},{17,1},{25,9},{2,18},{10... | collective-permute-start | bytes 1720328 | tf_op jit(solution)/shard_map/ppermute | solution.py:121
  249.2 32.1 %collective-permute-start.39 = (bf16[320,896]{1,0:T(8,128)(2,1)}, bf16[320,896]{1,0:T(8,128)(2,1)}, u32[]{:S(2)}, u32[]{:S(2)}) collective-permute-start(bf16[320,896]{1,0:T(8,128)(2,1)} %add.367), channel_id=1, source_target_pairs={{0,8},{8,0},{16,24},{24,16},{1,9},{9,1},{17,25},{25,17},{2,10},{10... | collective-permute-start | bytes 1720328 | tf_op jit(solution)/shard_map/ppermute | solution.py:122
  259.5 12.5 %collective-permute-start.40 = (bf16[192,896]{1,0:T(8,128)(2,1)S(1)}, bf16[192,896]{1,0:T(8,128)(2,1)S(1)}, u32[]{:S(2)}, u32[]{:S(2)}) collective-permute-start(bf16[192,896]{1,0:T(8,128)(2,1)S(1)} %copy-done.11), channel_id=1, source_target_pairs={{0,8},{8,0},{16,24},{24,16},{1,9},{9,1},{17,25},{25,17},{2,10},{10... | collective-permute-start | bytes 1032200 | tf_op jit(solution)/shard_map/ppermute | solution.py:111
  271.9 9.4 %collective-permute-start.41 = (bf16[192,896]{1,0:T(8,128)(2,1)S(1)}, bf16[192,896]{1,0:T(8,128)(2,1)S(1)}, u32[]{:S(2)}, u32[]{:S(2)}) collective-permute-start(bf16[192,896]{1,0:T(8,128)(2,1)S(1)} %copy-done.10), channel_id=1, source_target_pairs={{0,16},{8,24},{16,0},{24,8},{1,17},{9,25},{17,1},{25,9},{2,18},{10... | collective-permute-start | bytes 1032200 | tf_op jit(solution)/shard_map/ppermute | solution.py:112
  281.3 45.3 %collective-permute-start.49 = (bf16[240,4096]{1,0:T(8,128)(2,1)}, bf16[240,4096]{1,0:T(8,128)(2,1)}, u32[]{:S(2)}, u32[]{:S(2)}) collective-permute-start(bf16[240,4096]{1,0:T(8,128)(2,1)} %pad_maximum_fusion.1), channel_id=1, source_target_pairs={{0,2},{1,3},{2,0},{3,1},{4,6},{5,7},{6,4},{7,5},{8,10},{9,11},{10,... | collective-permute-start | bytes 5898248 | tf_op jit(solution)/shard_map/ppermute | solution.py:152
  283.7 38.0 %collective-permute-start.43 = (bf16[128,4096]{1,0:T(8,128)(2,1)}, bf16[128,4096]{1,0:T(8,128)(2,1)}, u32[]{:S(2)}, u32[]{:S(2)}) collective-permute-start(bf16[128,4096]{1,0:T(8,128)(2,1)} %slice_add_fusion.10), channel_id=1, source_target_pairs={{0,0},{1,1},{2,4},{3,5},{4,2},{5,3},{6,6},{7,7},{8,8},{9,9},{10,12... | collective-permute-start | bytes 3145736 | tf_op jit(solution)/shard_map/ppermute | solution.py:161
  298.6 12.9 %collective-permute-start.44 = (bf16[320,4096]{1,0:T(8,128)(2,1)}, bf16[320,4096]{1,0:T(8,128)(2,1)S(1)}, u32[]{:S(2)}, u32[]{:S(2)}) collective-permute-start(bf16[320,4096]{1,0:T(8,128)(2,1)} %convolution_convert_fusion.2), channel_id=1, source_target_pairs={{0,1},{1,0},{2,3},{3,2},{4,5},{5,4},{6,7},{7,6},{8,9},{9,8},{10,11... | collective-permute-start | bytes 7864328 | tf_op jit(solution)/shard_map/ppermute | solution.py:134
  299.4 22.2 %collective-permute-start.45 = (bf16[192,896]{1,0:T(8,128)(2,1)}, bf16[192,896]{1,0:T(8,128)(2,1)}, u32[]{:S(2)}, u32[]{:S(2)}) collective-permute-start(bf16[192,896]{1,0:T(8,128)(2,1)} %add.376), channel_id=1, source_target_pairs={{0,16},{8,24},{16,0},{24,8},{1,17},{9,25},{17,1},{25,9},{2,18},{10... | collective-permute-start | bytes 1032200 | tf_op jit(solution)/shard_map/ppermute | solution.py:121
  300.8 20.8 %collective-permute-start.46 = (bf16[192,896]{1,0:T(8,128)(2,1)}, bf16[192,896]{1,0:T(8,128)(2,1)}, u32[]{:S(2)}, u32[]{:S(2)}) collective-permute-start(bf16[192,896]{1,0:T(8,128)(2,1)} %add.377), channel_id=1, source_target_pairs={{0,8},{8,0},{16,24},{24,16},{1,9},{9,1},{17,25},{25,17},{2,10},{10... | collective-permute-start | bytes 1032200 | tf_op jit(solution)/shard_map/ppermute | solution.py:122
  321.6 55.4 %collective-permute-start.54 = (bf16[288,4096]{1,0:T(8,128)(2,1)}, bf16[288,4096]{1,0:T(8,128)(2,1)S(1)}, u32[]{:S(2)}, u32[]{:S(2)}) collective-permute-start(bf16[288,4096]{1,0:T(8,128)(2,1)} %pad_maximum_fusion), channel_id=1, source_target_pairs={{0,2},{1,3},{2,0},{3,1},{4,6},{5,7},{6,4},{7,5},{8,10},{9,11},{10,... | collective-permute-start | bytes 7077896 | tf_op jit(solution)/shard_map/ppermute | solution.py:152
  329.2 30.0 %collective-permute-start.50 = (bf16[160,4096]{1,0:T(8,128)(2,1)}, bf16[160,4096]{1,0:T(8,128)(2,1)}, u32[]{:S(2)}, u32[]{:S(2)}) collective-permute-start(bf16[160,4096]{1,0:T(8,128)(2,1)} %slice_add_fusion.6), channel_id=1, source_target_pairs={{0,0},{1,1},{2,4},{3,5},{4,2},{5,3},{6,6},{7,7},{8,8},{9,9},{10,12... | collective-permute-start | bytes 3932168 | tf_op jit(solution)/shard_map/ppermute | solution.py:161
  345.7 10.2 %collective-permute-start.51 = (bf16[192,4096]{1,0:T(8,128)(2,1)}, bf16[192,4096]{1,0:T(8,128)(2,1)}, u32[]{:S(2)}, u32[]{:S(2)}) collective-permute-start(bf16[192,4096]{1,0:T(8,128)(2,1)} %convolution_convert_fusion.8), channel_id=1, source_target_pairs={{0,1},{1,0},{2,3},{3,2},{4,5},{5,4},{6,7},{7,6},{8,9},{9,8},{10,11... | collective-permute-start | bytes 4718600 | tf_op jit(solution)/shard_map/ppermute | solution.py:134
  345.7 13.4 %collective-permute-start.52 = (bf16[64,896]{1,0:T(8,128)(2,1)S(1)}, bf16[64,896]{1,0:T(8,128)(2,1)S(1)}, u32[]{:S(2)}, u32[]{:S(2)}) collective-permute-start(bf16[64,896]{1,0:T(8,128)(2,1)S(1)} %add.386), channel_id=1, source_target_pairs={{0,16},{8,24},{16,0},{24,8},{1,17},{9,25},{17,1},{25,9},{2,18},{10... | collective-permute-start | bytes 344072 | tf_op jit(solution)/shard_map/ppermute | solution.py:121
  346.7 12.4 %collective-permute-start.53 = (bf16[64,896]{1,0:T(8,128)(2,1)S(1)}, bf16[64,896]{1,0:T(8,128)(2,1)S(1)}, u32[]{:S(2)}, u32[]{:S(2)}) collective-permute-start(bf16[64,896]{1,0:T(8,128)(2,1)S(1)} %add.387), channel_id=1, source_target_pairs={{0,8},{8,0},{16,24},{24,16},{1,9},{9,1},{17,25},{25,17},{2,10},{10... | collective-permute-start | bytes 344072 | tf_op jit(solution)/shard_map/ppermute | solution.py:122
  355.9 63.2 %collective-permute-start.57 = (bf16[240,4096]{1,0:T(8,128)(2,1)}, bf16[240,4096]{1,0:T(8,128)(2,1)S(1)}, u32[]{:S(2)}, u32[]{:S(2)}) collective-permute-start(bf16[240,4096]{1,0:T(8,128)(2,1)} %pad_maximum_fusion.2), channel_id=1, source_target_pairs={{0,2},{1,3},{2,0},{3,1},{4,6},{5,7},{6,4},{7,5},{8,10},{9,11},{10,... | collective-permute-start | bytes 5898248 | tf_op jit(solution)/shard_map/ppermute | solution.py:152
  378.4 15.3 %collective-permute-start.55 = (bf16[192,4096]{1,0:T(8,128)(2,1)}, bf16[192,4096]{1,0:T(8,128)(2,1)S(1)}, u32[]{:S(2)}, u32[]{:S(2)}) collective-permute-start(bf16[192,4096]{1,0:T(8,128)(2,1)} %slice_add_fusion.3), channel_id=1, source_target_pairs={{0,0},{1,1},{2,4},{3,5},{4,2},{5,3},{6,6},{7,7},{8,8},{9,9},{10,12... | collective-permute-start | bytes 4718600 | tf_op jit(solution)/shard_map/ppermute | solution.py:161
  383.6 8.1 %collective-permute-start.56 = (bf16[64,4096]{1,0:T(8,128)(2,1)}, bf16[64,4096]{1,0:T(8,128)(2,1)}, u32[]{:S(2)}, u32[]{:S(2)}) collective-permute-start(bf16[64,4096]{1,0:T(8,128)(2,1)} %convolution_convert_fusion.16), channel_id=1, source_target_pairs={{0,1},{1,0},{2,3},{3,2},{4,5},{5,4},{6,7},{7,6},{8,9},{9,8},{10,11... | collective-permute-start | bytes 1572872 | tf_op jit(solution)/shard_map/ppermute | solution.py:134
  386.0 76.7 %collective-permute-start.60 = (bf16[144,4096]{1,0:T(8,128)(2,1)}, bf16[144,4096]{1,0:T(8,128)(2,1)S(1)}, u32[]{:S(2)}, u32[]{:S(2)}) collective-permute-start(bf16[144,4096]{1,0:T(8,128)(2,1)} %pad_maximum_fusion.4), channel_id=1, source_target_pairs={{0,2},{1,3},{2,0},{3,1},{4,6},{5,7},{6,4},{7,5},{8,10},{9,11},{10,... | collective-permute-start | bytes 3538952 | tf_op jit(solution)/shard_map/ppermute | solution.py:152
  419.3 42.0 %collective-permute-start.59 = (bf16[160,4096]{1,0:T(8,128)(2,1)S(1)}, bf16[160,4096]{1,0:T(8,128)(2,1)S(1)}, u32[]{:S(2)}, u32[]{:S(2)}) collective-permute-start(bf16[160,4096]{1,0:T(8,128)(2,1)S(1)} %slice_add_fusion.5), channel_id=1, source_target_pairs={{0,0},{1,1},{2,4},{3,5},{4,2},{5,3},{6,6},{7,7},{8,8},{9,9},{10,12... | collective-permute-start | bytes 3932168 | tf_op jit(solution)/shard_map/ppermute | solution.py:161
  420.2 41.1 %collective-permute-start.58 = (bf16[96,4096]{1,0:T(8,128)(2,1)S(1)}, bf16[96,4096]{1,0:T(8,128)(2,1)S(1)}, u32[]{:S(2)}, u32[]{:S(2)}) collective-permute-start(bf16[96,4096]{1,0:T(8,128)(2,1)S(1)} %slice_add_fusion.16), channel_id=1, source_target_pairs={{2,0},{3,1},{4,6},{5,7},{10,8},{11,9},{12,14},{13,15},{18,16},{19,... | collective-permute-start | bytes 2359304 | tf_op jit(solution)/shard_map/ppermute | solution.py:165
  421.5 61.9 %collective-permute-start.64 = (bf16[48,4096]{1,0:T(8,128)(2,1)S(1)}, bf16[48,4096]{1,0:T(8,128)(2,1)S(1)}, u32[]{:S(2)}, u32[]{:S(2)}) collective-permute-start(bf16[48,4096]{1,0:T(8,128)(2,1)S(1)} %slice_add_fusion.22), channel_id=1, source_target_pairs={{0,2},{1,3},{2,0},{3,1},{4,6},{5,7},{6,4},{7,5},{8,10},{9,11},{10,... | collective-permute-start | bytes 1179656 | tf_op jit(solution)/shard_map/ppermute | solution.py:152
  461.4 20.6 %collective-permute-start.61 = (bf16[80,4096]{1,0:T(8,128)(2,1)S(1)}, bf16[80,4096]{1,0:T(8,128)(2,1)S(1)}, u32[]{:S(2)}, u32[]{:S(2)}) collective-permute-start(bf16[80,4096]{1,0:T(8,128)(2,1)S(1)} %slice_add_fusion.19), channel_id=1, source_target_pairs={{2,0},{3,1},{4,6},{5,7},{10,8},{11,9},{12,14},{13,15},{18,16},{19,... | collective-permute-start | bytes 1966088 | tf_op jit(solution)/shard_map/ppermute | solution.py:165
  462.8 19.2 %collective-permute-start.62 = (bf16[96,4096]{1,0:T(8,128)(2,1)S(1)}, bf16[96,4096]{1,0:T(8,128)(2,1)S(1)}, u32[]{:S(2)}, u32[]{:S(2)}) collective-permute-start(bf16[96,4096]{1,0:T(8,128)(2,1)S(1)} %slice_add_fusion.11), channel_id=1, source_target_pairs={{0,0},{1,1},{2,4},{3,5},{4,2},{5,3},{6,6},{7,7},{8,8},{9,9},{10,12... | collective-permute-start | bytes 2359304 | tf_op jit(solution)/shard_map/ppermute | solution.py:161
  482.1 11.3 %collective-permute-start.63 = (bf16[48,4096]{1,0:T(8,128)(2,1)S(1)}, bf16[48,4096]{1,0:T(8,128)(2,1)S(1)}, u32[]{:S(2)}, u32[]{:S(2)}) collective-permute-start(bf16[48,4096]{1,0:T(8,128)(2,1)S(1)} %slice_add_fusion.26), channel_id=1, source_target_pairs={{2,0},{3,1},{4,6},{5,7},{10,8},{11,9},{12,14},{13,15},{18,16},{19,... | collective-permute-start | bytes 1179656 | tf_op jit(solution)/shard_map/ppermute | solution.py:165
  493.3 6.9 %collective-permute-start.66 = (bf16[16,4096]{1,0:T(8,128)(2,1)S(1)}, bf16[16,4096]{1,0:T(8,128)(2,1)S(1)}, u32[]{:S(2)}, u32[]{:S(2)}) collective-permute-start(bf16[16,4096]{1,0:T(8,128)(2,1)S(1)} %slice_add_fusion.30), channel_id=1, source_target_pairs={{2,0},{3,1},{4,6},{5,7},{10,8},{11,9},{12,14},{13,15},{18,16},{19,... | collective-permute-start | bytes 393224 | tf_op jit(solution)/shard_map/ppermute | solution.py:165
  (46 other events, 446.7 us)
